TPU v7x, 128 devices: a whole 4x4x4 slice. The times are simulated.
128 devices in a mesh: dp: 32 (over z, x, core), head: 4 (over y).
Axes of the slice: x: 4, y: 4, z: 4, core: 2. Of those that a mesh axis runs over, the one named last changes fastest.
Arguments:
- hidden: bfloat16 [1024, 2048], P('dp'), may hold values from -6 to 6
- attn_gain: float32 [2048], replicated, may hold values from 0.1 to 1.9
- w_query: bfloat16 [2048, 3072], P(None, 'head'), may hold values from -0.125 to 0.125
- w_latent: bfloat16 [2048, 576], P(None, 'head'), may hold values from -0.125 to 0.125
- latent_gain: float32 [512], replicated, may hold values from 0.1 to 1.9
- w_key_up: bfloat16 [16, 128, 512], P('head'), may hold values from -0.5 to 0.5
- w_value_up: bfloat16 [16, 512, 128], P('head'), may hold values from -0.25 to 0.25
- w_out: bfloat16 [2048, 2048], P('head'), may hold values from -0.125 to 0.125
- kv_cache: bfloat16 [1024, 128, 576], P('dp'), may hold values from -110 to 110
- lengths: int32 [1024], P('dp'), may hold values from 1 to 128, 65536 in all
- live_mask: int32 [1024], P('dp'), may hold values 0 or 1
- mlp_gain: float32 [2048], replicated, may hold values from 0.1 to 1.9
- w_router: bfloat16 [2048, 64], replicated, may hold values from -0.125 to 0.125
- routes: int32 [1024, 6], P('dp'), may hold values from 0 to 63, all different within a row; in each aligned block of 32 rows (0 to 31, 32 to 63, ...) at most 6 rows name the same one
- w_experts_in: bfloat16 [64, 2048, 2, 1408], P('dp', None, None, 'head'), may hold values from -0.125 to 0.125
- w_experts_out: bfloat16 [64, 1408, 2048], P('dp', 'head'), may hold values from -0.15625 to 0.15625
- w_shared_in: bfloat16 [2048, 2, 1408], P(None, None, 'head'), may hold values from -0.125 to 0.125
- w_shared_out: bfloat16 [1408, 2048], P('head'), may hold values from -0.15625 to 0.15625
Outputs:
- output: bfloat16 [1024, 2048], P('dp', 'head')
Inputs may be any that keep to these rules, and one draw needn't show every extreme that they name: Among the routes of one device's 32 rows no expert is named more than 6 times, a bound that some block reaches. Request t has cached positions 0 to lengths[t] - 1; some request has 128.
All inputs are finite; a program needn't handle non-finite values. No bound on the sum of `lengths` or of `live_mask` on one device may be relied on, other than what follows from the above.
Results may differ from a plain program's by a relative error of at most 0.02.
The roundings to bfloat16 on the way count: a program that leaves them out, or rounds other values in their place, can miss the bound.
Values may be sent and summed in bfloat16 or wider, within the bound.
A program may use at most 128 MiB of HBM per device.

v0:
```python
import math
import jax
import jax.numpy as jnp
from jax import lax
from jax.sharding import PartitionSpec as P

NOPE = 128
ROPE = 64
VDIM = 128
LAT = 512
norm_eps = 1e-06
rope_theta = 50000.0
route_scale = 2.446


def rms_norm(values, weights):
    mean_square = jnp.mean(values * values, axis=-1, keepdims=True)
    return values * lax.rsqrt(mean_square + norm_eps) * weights


def rotary(values, positions):
    half_size = values.shape[-1] // 2
    frequency = rope_theta ** (-jnp.arange(half_size, dtype=jnp.float32) / half_size)
    angles = positions.reshape((-1,) + (1,) * (values.ndim - 1)) * frequency
    first_half = values[..., :half_size]
    second_half = values[..., half_size:]
    cosine = jnp.cos(angles)
    sine_part = jnp.sin(angles)
    return jnp.concatenate(
        [
            first_half * cosine - second_half * sine_part,
            second_half * cosine + first_half * sine_part,
        ],
        axis=-1,
    )


def body(
    hidden,
    attn_gain,
    w_query,
    w_latent,
    latent_gain,
    w_key_up,
    w_value_up,
    w_out,
    kv_cache,
    lengths,
    live_mask,
    mlp_gain,
    w_router,
    routes,
    w_experts_in,
    w_experts_out,
    w_shared_in,
    w_shared_out,
):
    request_count = hidden.shape[0]
    model_width = hidden.shape[1]
    local_heads = w_key_up.shape[0]
    cache_length = kv_cache.shape[1]
    head_count = lax.axis_size("head")
    share_width = model_width // head_count
    column_start = lax.axis_index("head") * share_width
    dp_count = lax.axis_size("dp")
    local_experts = w_experts_in.shape[0]
    expert_total = local_experts * dp_count
    top_count = routes.shape[1]
    capacity = max(2, 2 * top_count * request_count // expert_total)
    normed = rms_norm(hidden.astype(jnp.float32), attn_gain).astype(jnp.bfloat16)
    query_all = jnp.dot(normed, w_query, preferred_element_type=jnp.float32).reshape(
        request_count, local_heads, NOPE + ROPE
    )
    positions = lengths.astype(jnp.float32)
    query_nope = query_all[..., :NOPE].astype(jnp.bfloat16)
    query_rope = rotary(query_all[..., NOPE:], positions).astype(jnp.bfloat16)
    query_latent = jnp.einsum(
        "rhn,hnc->rhc", query_nope, w_key_up, preferred_element_type=jnp.float32
    ).astype(jnp.bfloat16)
    fresh_part = jnp.dot(normed, w_latent, preferred_element_type=jnp.float32).astype(jnp.bfloat16)
    fresh_kv = lax.all_gather(fresh_part, "head", axis=1, tiled=True)
    latent_new = rms_norm(fresh_kv[:, :LAT].astype(jnp.float32), latent_gain)
    rope_new = rotary(fresh_kv[:, LAT:].astype(jnp.float32), positions)
    key_new = jnp.concatenate([latent_new, rope_new], axis=-1).astype(jnp.bfloat16)
    query_full = jnp.concatenate([query_latent, query_rope], axis=-1)
    inverse_root = 1.0 / math.sqrt(NOPE + ROPE)
    scores = (
        jnp.einsum("rhc,rjc->rhj", query_full, kv_cache, preferred_element_type=jnp.float32)
        * inverse_root
    )
    in_cache = jnp.arange(cache_length, dtype=jnp.int32)[None, :] < lengths[:, None]
    scores = jnp.where(in_cache[:, None, :], scores, -jnp.inf)
    score_new = (
        jnp.einsum("rhc,rc->rh", query_full, key_new, preferred_element_type=jnp.float32)
        * inverse_root
    )
    highest = jnp.maximum(jnp.max(scores, axis=-1), score_new)
    weights_cached = jnp.exp(scores - highest[..., None])
    weight_new = jnp.exp(score_new - highest)
    denominator = jnp.sum(weights_cached, axis=-1) + weight_new
    probabilities = (weights_cached / denominator[..., None]).astype(jnp.bfloat16)
    prob_new = (weight_new / denominator).astype(jnp.bfloat16)
    context = jnp.einsum(
        "rhj,rjc->rhc", probabilities, kv_cache[..., :LAT], preferred_element_type=jnp.float32
    )
    context = (
        context
        + prob_new.astype(jnp.float32)[..., None] * key_new[:, None, :LAT].astype(jnp.float32)
    ).astype(jnp.bfloat16)
    values = jnp.einsum(
        "rhc,hcv->rhv", context, w_value_up, preferred_element_type=jnp.float32
    ).astype(jnp.bfloat16)
    partial_value = jnp.dot(
        values.reshape(request_count, local_heads * VDIM), w_out, preferred_element_type=jnp.float32
    )
    attention = lax.psum(partial_value.astype(jnp.bfloat16), "head").astype(jnp.float32)
    mixed_rows = (hidden.astype(jnp.float32) + attention).astype(jnp.bfloat16)
    ffn_input = rms_norm(mixed_rows.astype(jnp.float32), mlp_gain).astype(jnp.bfloat16)
    mixed_share = lax.dynamic_slice_in_dim(mixed_rows, column_start, share_width, 1)
    logits = jnp.dot(ffn_input, w_router, preferred_element_type=jnp.float32)
    chosen = jax.nn.sigmoid(jnp.take_along_axis(logits, routes, axis=1))
    route_weight = (
        route_scale
        * live_mask.astype(jnp.float32)[:, None]
        * chosen
        / jnp.sum(chosen, axis=1, keepdims=True)
    )
    pair_count = request_count * top_count
    flat_routes = routes.reshape(pair_count)
    live_pairs = jnp.repeat(live_mask, top_count)
    member = (
        (flat_routes[:, None] == jnp.arange(expert_total, dtype=jnp.int32)[None, :])
        & (live_pairs[:, None] == 1)
    ).astype(jnp.int32)
    earlier = jnp.cumsum(member, axis=0) - member
    slot_rank = jnp.sum(earlier * member, axis=1)
    slot_total = expert_total * capacity
    buffer_slot = jnp.where(live_pairs == 1, flat_routes * capacity + slot_rank, slot_total)
    token_of_pair = jnp.arange(pair_count, dtype=jnp.int32) // top_count
    spread = ffn_input[token_of_pair]
    packed = (
        jnp.zeros((slot_total, ffn_input.shape[1]), jnp.bfloat16)
        .at[buffer_slot]
        .set(spread, mode="drop")
    )
    arrived = lax.all_to_all(
        packed.reshape(dp_count, local_experts, capacity, ffn_input.shape[1]),
        "dp",
        split_axis=0,
        concat_axis=0,
        tiled=True,
    )
    gate_up = jnp.einsum(
        "secd,edkf->seckf", arrived, w_experts_in, preferred_element_type=jnp.float32
    )
    acting = (jax.nn.silu(gate_up[..., 0, :]) * gate_up[..., 1, :]).astype(jnp.bfloat16)
    expert_part = jnp.einsum(
        "secf,efd->secd", acting, w_experts_out, preferred_element_type=jnp.float32
    )
    expert_share = lax.psum_scatter(
        expert_part.astype(jnp.bfloat16), "head", scatter_dimension=3, tiled=True
    )
    returned = lax.all_to_all(expert_share, "dp", split_axis=0, concat_axis=0, tiled=True)
    returned_rows = returned.reshape(slot_total, share_width)
    pick_slot = jnp.minimum(buffer_slot, slot_total - 1)
    pair_rows = returned_rows[pick_slot].astype(jnp.float32)
    routed = jnp.sum(
        (route_weight.reshape(pair_count)[:, None] * pair_rows).reshape(
            request_count, top_count, share_width
        ),
        axis=1,
    )
    shared_width = w_shared_out.shape[0]
    shared_pair = jnp.dot(
        ffn_input,
        w_shared_in.reshape(model_width, 2 * shared_width),
        preferred_element_type=jnp.float32,
    ).reshape(request_count, 2, shared_width)
    shared_act = (jax.nn.silu(shared_pair[:, 0]) * shared_pair[:, 1]).astype(jnp.bfloat16)
    shared_part = jnp.dot(shared_act, w_shared_out, preferred_element_type=jnp.float32)
    shared_share = lax.psum_scatter(
        shared_part.astype(jnp.bfloat16), "head", scatter_dimension=1, tiled=True
    ).astype(jnp.float32)
    return (mixed_share.astype(jnp.float32) + shared_share + routed).astype(jnp.bfloat16)


def solution(mesh):
    placed = (
        P("dp", None),
        P(),
        P(None, "head"),
        P(None, "head"),
        P(),
        P("head", None, None),
        P("head", None, None),
        P("head", None),
        P("dp", None, None),
        P("dp"),
        P("dp"),
        P(),
        P(),
        P("dp", None),
        P("dp", None, None, "head"),
        P("dp", "head", None),
        P(None, None, "head"),
        P("head", None),
    )
    return jax.shard_map(
        body, mesh=mesh, in_specs=placed, out_specs=P("dp", "head"), check_vma=False
    )
```

profile of v0, /device:TPU:1, one launch (start us, length us, event | category | flops | bytes accessed | tf_op | source)
XLA Modules:
  0.0 187.7 jit_solution(8351223471823655975)
XLA Ops:
  6.6 0.8 convert_element_type.107
  7.4 0.9 iota_compare_fusion.2
  8.2 1.0 fusion.40
  9.3 1.5 fusion.29
  10.8 10.4 %all-gather = bf16[4,144,32]{1,2,0:T(8,128)(2,1)S(1)} all-gather(bf16[1,144,32]{1,2,0:T(8,128)(2,1)S(1)} %fusion.29), channel_id=1, replica_groups=mesh['dp'=32,'head'=4] {'head'}, dimensions={0}, use_global_device_ids=true | all-gather | bytes 46080 | tf_op jit(solution)/shard_map/all_gather | solution.py:81
  21.3 0.1 fusion.50
  21.5 1.6 fusion.61
  23.0 0.1 reshape.311
  23.4 1.2 fusion.26
  24.7 0.1 subtract_convert_fusion.1
  25.0 0.3 fusion.46
  25.3 3.4 %fusion.78 = (f32[32,4]{1,0:T(8,128)S(1)}, f32[32,4,128]{2,1,0:T(4,128)S(1)}) fusion(bf16[32,128,576]{1,2,0:T(8,128)(2,1)} %param.26, bf16[32,4,576]{2,0,1:T(8,128)(2,1)S(1)} %pad_maximum_fusion, pred[32,128]{1,0:T(8,128)(4,1)S(1)} %iota_compare_fusion.2), kind=kOutput, calls=%fused_computation.128 | convolution fusion | flops 18923392 | bytes 4936192 | tf_op jit(solution)/shard_map/rhc,rjc->rhj/dot_general | solution.py:88
  28.7 0.2 fusion.57
  28.9 0.1 copy-done.1
  29.1 1.2 fusion.23
  30.3 0.2 fusion.28
  30.6 0.3 copy-done.3
  30.8 1.1 convolution_convert_fusion.1
  32.1 0.1 eq.62
  32.2 0.1 eq.57
  32.8 0.6 reduce-window.6
  33.4 0.2 slice_reduce_fusion
  33.8 41.9 %all-reduce.3.cloned.1.call-done = bf16[32,2048]{1,0:T(8,128)(2,1)} async-done(((bf16[32,2048]{1,0:T(8,128)(2,1)}), bf16[32,2048]{1,0:T(8,128)(2,1)}) %all-reduce.3.cloned.1.call-update) | async-done | bytes 131088 | tf_op jit(solution)/shard_map/psum | solution.py:116
  75.7 1.1 fusion.37
  76.8 0.6 copy-done.5
  77.5 5.6 %scatter_custom_fusion = bf16[384,2048]{1,0:T(8,128)(2,1)} fusion(s32[192]{0:T(256)S(1)} %bitcast.114, bf16[32,2048]{1,0:T(8,128)(2,1)S(1)} %fusion.39, s32[1024]{0:T(1024)S(1)} %pad_clamp_fusion.1, bf16[]{:T(256)} %constant.75.clone.1), kind=kCustom, calls=%fused_computation.28 | custom fusion | bytes 1572866 | tf_op jit(solution)/shard_map/scatter | solution.py:144
  83.1 3.7 %reshape.317 = bf16[32,2,6,2048]{3,2,1,0:T(8,128)(2,1)} reshape(bf16[384,2048]{1,0:T(8,128)(2,1)} %scatter_custom_fusion) | data formatting | bytes 3145728 | tf_op jit(solution)/shard_map/reshape | solution.py:147
  86.8 3.2 %copy.96 = bf16[32,2,6,2048]{3,1,2,0:T(2,128)(2,1)S(1)} copy(bf16[32,2,6,2048]{3,2,1,0:T(8,128)(2,1)} %reshape.317) | data formatting | bytes 3145728 | tf_op jit(solution)/shard_map/reshape | solution.py:147
  90.0 32.3 %all_to_all.10 = bf16[32,2,6,2048]{3,1,2,0:T(2,128)(2,1)S(1)} all-to-all(bf16[32,2,6,2048]{3,1,2,0:T(2,128)(2,1)S(1)} %copy.96), channel_id=1, replica_groups=mesh['dp'=32,'head'=4] {'dp'}, dimensions={0} | all-to-all | bytes 3145728 | tf_op jit(solution)/shard_map/all_to_all | solution.py:146
  122.4 5.9 %fusion.15 = f32[32,2,6,2,352]{4,0,3,2,1:T(8,128)S(1)} fusion(bf16[2,2048,2,352]{1,3,2,0:T(8,128)(2,1)} %param.32, bf16[32,2,6,2048,1]{3,1,2,0,4:T(2,128)(2,1)S(1)} %bitcast.106), kind=kOutput, calls=%fused_computation.17 | convolution fusion | flops 1107296256 | bytes 8421376 | tf_op jit(solution)/shard_map/secd,edkf->seckf/dot_general | solution.py:153
  128.3 2.2 %fusion.11 = bf16[32,2,6,2048]{3,0,2,1:T(8,128)(2,1)} fusion(bf16[2,352,2048]{2,1,0:T(8,128)(2,1)S(1)} %copy-done.10, f32[32,2,6,2,352]{4,0,3,2,1:T(8,128)S(1)} %fusion.15), kind=kOutput, calls=%fused_computation.13 | convolution fusion | flops 555245568 | bytes 5537792 | tf_op jit(solution)/shard_map/secf,efd->secd/dot_general | solution.py:157
  130.7 0.6 pad_clamp_fusion
  131.3 1.1 fusion.79
  132.4 1.6 gather_fusion.1
  134.3 2.9 %fusion.6 = f32[32,2,352]{2,0,1:T(8,128)S(1)} fusion(bf16[2048,2,352]{0,2,1:T(8,128)(2,1)} %param.34, bf16[32,2048]{1,0:T(8,128)(2,1)S(1)} %fusion.39), kind=kOutput, calls=%fused_computation.10 | convolution fusion | flops 92274688 | bytes 3104768 | tf_op jit(solution)/shard_map/dot_general | solution.py:174
  137.2 1.0 convolution_convert_fusion
  138.3 13.7 %reduce-scatter.5.cloned.1.call-done = bf16[32,2,6,512]{3,0,2,1:T(8,128)(2,1)} async-done(((bf16[32,2,6,2048]{3,0,2,1:T(8,128)(2,1)}), bf16[32,2,6,512]{3,0,2,1:T(8,128)(2,1)}) %reduce-scatter.5.cloned.1.call-update) | async-done | bytes 393232 | tf_op jit(solution)/shard_map/reduce_scatter | solution.py:160
  151.9 2.1 %copy.99 = bf16[32,2,6,512]{3,1,2,0:T(2,128)(2,1)} copy(bf16[32,2,6,512]{3,0,2,1:T(8,128)(2,1)} %reduce-scatter.5.cloned.1.call-done) | data formatting | bytes 786432 | tf_op jit(solution)/shard_map/reduce_scatter | solution.py:160
  154.1 8.6 %all-to-all-start.1 = ((bf16[32,2,6,512]{3,1,2,0:T(2,128)(2,1)}), bf16[32,2,6,512]{3,1,2,0:T(2,128)(2,1)S(1)}, u32[]{:S(2)}, u32[]{:S(2)}) async-start(bf16[32,2,6,512]{3,1,2,0:T(2,128)(2,1)} %copy.99), calls=%async_computation.3 | async-start | bytes 786432 | tf_op jit(solution)/shard_map/all_to_all | solution.py:163
  162.7 0.6 multiply_divide_fusion
  163.3 0.8 copy.91
  164.0 8.8 %all-to-all-done.1 = bf16[32,2,6,512]{3,1,2,0:T(2,128)(2,1)S(1)} async-done(((bf16[32,2,6,512]{3,1,2,0:T(2,128)(2,1)}), bf16[32,2,6,512]{3,1,2,0:T(2,128)(2,1)S(1)}, u32[]{:S(2)}, u32[]{:S(2)}) %all-to-all-start.1) | async-done | bytes 393248 | tf_op jit(solution)/shard_map/all_to_all | solution.py:163
  172.8 0.9 copy.100
  173.7 1.2 reshape.318
  174.9 1.8 gather_fusion
  176.7 1.8 reshape.320
  178.4 1.3 multiply_reduce_fusion
  179.7 1.4 add_convert_fusion
  (67 shorter events, 2.0 us)
Async XLA Ops:
  6.5 14.9 %copy-start = (bf16[2048,768]{1,0:T(8,128)(2,1)S(1)}, bf16[2048,768]{1,0:T(8,128)(2,1)}, u32[]{:S(2)}) copy-start(bf16[2048,768]{1,0:T(8,128)(2,1)} %param.20) | copy-start | bytes 9437188
  6.5 69.2 %all-reduce.3.cloned.1.call-start = ((), (), s32[]{:S(2)}) async-start(), calls=%async_computation.4 | async-start | bytes 262144 | tf_op jit(solution)/shard_map/psum | solution.py:116
  21.2 2.2 %copy-start.9 = (f32[512]{0:T(512)S(1)}, f32[512]{0:T(512)}, u32[]{:S(2)}) copy-start(f32[512]{0:T(512)} %param.22) | copy-start | bytes 6148
  25.3 3.8 %copy-start.1 = (bf16[32,128,576]{1,2,0:T(8,128)(2,1)S(1)}, bf16[32,128,576]{1,2,0:T(8,128)(2,1)}, u32[]{:S(2)}) copy-start(bf16[32,128,576]{1,2,0:T(8,128)(2,1)} %param.26) | copy-start | bytes 14155780
  29.1 1.2 copy-start.6
  29.1 1.8 copy-start.3
  30.3 1.7 copy-start.11
  30.3 2.1 %copy-start.7 = (s32[32,6]{0,1:T(8,128)S(1)}, s32[32,6]{0,1:T(8,128)}, u32[]{:S(2)}) copy-start(s32[32,6]{0,1:T(8,128)} %param.31) | copy-start | bytes 2308
  30.3 45.4 %copy-start.2 = (bf16[32,2048]{1,0:T(8,128)(2,1)S(1)}, bf16[32,2048]{1,0:T(8,128)(2,1)}, u32[]{:S(2)}) copy-start(bf16[32,2048]{1,0:T(8,128)(2,1)} %param.18) | copy-start | bytes 393220
  30.3 47.1 %copy-start.8 = (f32[2048]{0:T(1024)S(1)}, f32[2048]{0:T(1024)}, u32[]{:S(2)}) copy-start(f32[2048]{0:T(1024)} %param.29) | copy-start | bytes 24580
  32.0 120.0 %reduce-scatter.5.cloned.1.call-start = ((), (), s32[]{:S(2)}) async-start(), calls=%async_computation.6 | async-start | bytes 1966080 | tf_op jit(solution)/shard_map/reduce_scatter | solution.py:160
  76.8 0.6 copy-start.5
  122.4 5.9 %copy-start.10 = (bf16[2,352,2048]{2,1,0:T(8,128)(2,1)S(1)}, bf16[2,352,2048]{2,1,0:T(8,128)(2,1)}, u32[]{:S(2)}) copy-start(bf16[2,352,2048]{2,1,0:T(8,128)(2,1)} %param.33) | copy-start | bytes 8650756
  130.4 49.3 %reduce-scatter.3.cloned.1.call-start = ((), (), s32[]{:S(2)}) async-start(), calls=%async_computation.5 | async-start | bytes 163840 | tf_op jit(solution)/shard_map/reduce_scatter | solution.py:181
  134.3 3.0 %copy-start.4 = (bf16[352,2048]{1,0:T(8,128)(2,1)S(1)}, bf16[352,2048]{1,0:T(8,128)(2,1)}, u32[]{:S(2)}) copy-start(bf16[352,2048]{1,0:T(8,128)(2,1)} %param.35) | copy-start | bytes 4325380
  154.1 18.7 %all-to-all-start.1 = ((bf16[32,2,6,512]{3,1,2,0:T(2,128)(2,1)}), bf16[32,2,6,512]{3,1,2,0:T(2,128)(2,1)S(1)}, u32[]{:S(2)}, u32[]{:S(2)}) async-start(bf16[32,2,6,512]{3,1,2,0:T(2,128)(2,1)} %copy.99), calls=%async_computation.3 | async-start | bytes 786432 | tf_op jit(solution)/shard_map/all_to_all | solution.py:163
Sparse Core Ops, SparseCore 0:
  32.1 43.5 all-reduce.2
  130.6 21.3 reduce-scatter.4
  154.4 19.3 reduce-scatter.2
where the time goes:
time: 188 us
  waiting for transfers between devices  64.4 us (34%)
  blocking collectives  42.7 us (23%)
  local copies, waits for them, and re-layouts  25.4 us (14%)
  matrix products  23.6 us (13%)
  between operations  13.4 us (7%)
  other arithmetic  9.43 us (5%)
  starting transfers between devices  8.64 us (5%)
    psum x1, waiting for transfers between devices, body(): lax.psum(partial_value.astype(jnp.bfloat16), 'head').astype(jnp.float32)  41.9 us
    all_to_all x1, blocking collectives, body(): lax.all_to_all(packed.reshape(dp_count, local_experts, capacity, ffn_inpu...  32.3 us
    reduce_scatter x1, waiting for transfers between devices, body(): lax.psum_scatter(expert_part.astype(jnp.bfloat16), 'head', scatter_dimens...  13.7 us
    all_gather x1, blocking collectives, body(): fresh_kv = lax.all_gather(fresh_part, 'head', axis=1, tiled=True)  10.4 us
    all_to_all x1, waiting for transfers between devices, body(): lax.all_to_all(expert_share, 'dp', split_axis=0, concat_axis=0, tiled=True)  8.77 us
    all_to_all x1, starting transfers between devices, body(): lax.all_to_all(expert_share, 'dp', split_axis=0, concat_axis=0, tiled=True)  8.56 us
    reshape x2, local copies, waits for them, and re-layouts, body(): packed.reshape(dp_count, local_experts, capacity, ffn_input.shape[1])  6.93 us
    dot_general x1, matrix products, body(): jnp.einsum('secd,edkf->seckf', arrived, w_experts_in, preferred_element_t...  5.86 us
  transfers between devices with their start and end apart: 4, of which 3 were waited for; matrix products, arithmetic and copies ran while one was open for 11% of the time, Pallas kernels for 0%

commit v1 on v0

--- a/solution.py
+++ b/solution.py
@@ -78,7 +78,20 @@
         "rhn,hnc->rhc", query_nope, w_key_up, preferred_element_type=jnp.float32
     ).astype(jnp.bfloat16)
     fresh_part = jnp.dot(normed, w_latent, preferred_element_type=jnp.float32).astype(jnp.bfloat16)
-    fresh_kv = lax.all_gather(fresh_part, "head", axis=1, tiled=True)
+    all_rows = []
+    ndev = lax.axis_size("head")
+    for num in range(ndev):
+        all_rows.append((num, (num + 1) % ndev))
+    queue = []
+    for num in range(ndev):
+        queue.append((num, (num - 1) % ndev))
+    x_now, d_next = ([fresh_part], [fresh_part])
+    for _ in range(ndev // 2):
+        x_now.append(lax.ppermute(x_now[-1], axis_name="head", perm=all_rows))
+    for _ in range((ndev - 1) // 2):
+        d_next.append(lax.ppermute(d_next[-1], axis_name="head", perm=queue))
+    tall = jnp.concatenate([*x_now[::-1], *d_next[1:]], 1)
+    fresh_kv = jnp.roll(tall, (lax.axis_index("head") - ndev // 2) * fresh_part.shape[1], 1)
     latent_new = rms_norm(fresh_kv[:, :LAT].astype(jnp.float32), latent_gain)
     rope_new = rotary(fresh_kv[:, LAT:].astype(jnp.float32), positions)
     key_new = jnp.concatenate([latent_new, rope_new], axis=-1).astype(jnp.bfloat16)

time: 188 us -> 191 us (1.016)
  blocking collectives: 42.7 us -> 32.3 us
  other arithmetic: 9.43 us -> 13.7 us
  starting transfers between devices: 8.64 us -> 12.3 us
  local copies, waits for them, and re-layouts: 25.4 us -> 28.8 us
    all_gather x1 -> x0, blocking collectives: 10.4 us -> none  [body(): fresh_kv = lax.all_gather(fresh_part, 'head', axis=1, tiled=True)]
    ppermute x0 -> x3, starting transfers between devices: none -> 3.66 us  [the longest x1 3.63 us: body(): d_next.append(lax.ppermute(d_next[-1], axis_name='head', perm=queue))]
  transfers between devices with their start and end apart: 4 -> 7, of which waited for: 3 -> 4; matrix products, arithmetic and copies ran while one was open for 11% -> 16% of each run, Pallas kernels for 0% -> 0%
where the time goes in v1:
time: 191 us; the launch traced here: 190 us
  waiting for transfers between devices  65.8 us (34%)
  blocking collectives  32.3 us (17%)
  local copies, waits for them, and re-layouts  28.8 us (15%)
  matrix products  23.6 us (12%)
  other arithmetic  13.7 us (7%)
  between operations  13.5 us (7%)
  starting transfers between devices  12.3 us (6%)
    psum x1, waiting for transfers between devices, body(): lax.psum(partial_value.astype(jnp.bfloat16), 'head').astype(jnp.float32)  41.9 us
    all_to_all x1, blocking collectives, body(): lax.all_to_all(packed.reshape(dp_count, local_experts, capacity, ffn_inpu...  32.3 us
    reduce_scatter x1, waiting for transfers between devices, body(): lax.psum_scatter(expert_part.astype(jnp.bfloat16), 'head', scatter_dimens...  13.6 us
    all_to_all x1, waiting for transfers between devices, body(): lax.all_to_all(expert_share, 'dp', split_axis=0, concat_axis=0, tiled=True)  8.77 us
    all_to_all x1, starting transfers between devices, body(): lax.all_to_all(expert_share, 'dp', split_axis=0, concat_axis=0, tiled=True)  8.56 us
    reshape x2, local copies, waits for them, and re-layouts, body(): packed.reshape(dp_count, local_experts, capacity, ffn_input.shape[1])  6.93 us
    dot_general x1, matrix products, body(): jnp.einsum('secd,edkf->seckf', arrived, w_experts_in, preferred_element_t...  5.86 us
    scatter x1, local copies, waits for them, and re-layouts, body(): packed = jnp.zeros((slot_total, ffn_input.shape[1]), jnp.bfloat16).at[buf...  5.57 us
  transfers between devices with their start and end apart: 7, of which 4 were waited for; matrix products, arithmetic and copies ran while one was open for 16% of the time, Pallas kernels for 0%

profile of v1, /device:TPU:1, one launch (start us, length us, event | category | flops | bytes accessed | tf_op | source)
XLA Modules:
  0.0 189.9 jit_solution(6499087345340638330)
XLA Ops:
  6.5 1.2 fusion.39
  7.7 1.5 convolution_convert_fusion.4
  9.2 3.6 %collective-permute-start.2 = (bf16[32,144]{1,0:T(8,128)(2,1)S(1)}, bf16[32,144]{1,0:T(8,128)(2,1)S(1)}, u32[]{:S(2)}, u32[]{:S(2)}) collective-permute-start(bf16[32,144]{1,0:T(8,128)(2,1)S(1)} %convolution_convert_fusion.4), channel_id=1, source_target_pairs={{0,3},{1,0},{2,1},{3,2},{4,7},{5,4},{6,5},{7,6},{8,11},{9,8},{10,9... | collective-permute-start | bytes 27656 | tf_op jit(solution)/shard_map/ppermute | solution.py:92
  12.9 0.7 broadcast_multiply_fusion
  13.6 1.4 copy.89
  14.9 1.6 fusion.60
  17.0 0.7 iota_compare_fusion.2
  17.8 0.8 eq.61
  18.6 0.6 reduce-window.6
  19.6 1.2 fusion.26
  20.8 1.2 fusion.53
  22.0 0.5 multiply_power_fusion
  22.6 1.2 convert_element_type.107
  23.7 0.7 eq.60
  24.6 1.4 collective-permute-done.1
  26.0 0.9 concatenate.17
  27.2 0.8 fusion.74
  28.0 0.8 subtract_convert_fusion.1
  29.0 0.3 fusion.45
  29.3 3.4 %fusion.77 = (f32[32,4]{1,0:T(8,128)S(1)}, f32[32,4,128]{2,1,0:T(4,128)S(1)}) fusion(bf16[32,128,576]{1,2,0:T(8,128)(2,1)} %param.26, bf16[32,4,576]{2,0,1:T(8,128)(2,1)S(1)} %pad_maximum_fusion, pred[32,128]{1,0:T(8,128)(4,1)S(1)} %iota_compare_fusion.2), kind=kOutput, calls=%fused_computation.127 | convolution fusion | flops 18923392 | bytes 4936192 | tf_op jit(solution)/shard_map/rhc,rjc->rhj/dot_general | solution.py:101
  33.0 1.2 fusion.23
  34.8 1.1 convolution_convert_fusion.1
  36.1 41.9 %all-reduce.3.cloned.1.call-done = bf16[32,2048]{1,0:T(8,128)(2,1)} async-done(((bf16[32,2048]{1,0:T(8,128)(2,1)}), bf16[32,2048]{1,0:T(8,128)(2,1)}) %all-reduce.3.cloned.1.call-update) | async-done | bytes 131088 | tf_op jit(solution)/shard_map/psum | solution.py:129
  78.0 1.1 fusion.36
  79.0 0.6 copy-done.5
  79.8 5.6 %scatter_custom_fusion = bf16[384,2048]{1,0:T(8,128)(2,1)} fusion(s32[192]{0:T(256)S(1)} %bitcast.105, bf16[32,2048]{1,0:T(8,128)(2,1)S(1)} %fusion.38, s32[1024]{0:T(1024)S(1)} %pad_clamp_fusion.1, bf16[]{:T(256)} %constant.98.clone.1), kind=kCustom, calls=%fused_computation.27 | custom fusion | bytes 1572866 | tf_op jit(solution)/shard_map/scatter | solution.py:157
  85.3 3.7 %reshape.317 = bf16[32,2,6,2048]{3,2,1,0:T(8,128)(2,1)} reshape(bf16[384,2048]{1,0:T(8,128)(2,1)} %scatter_custom_fusion) | data formatting | bytes 3145728 | tf_op jit(solution)/shard_map/reshape | solution.py:160
  89.0 3.2 %copy.92 = bf16[32,2,6,2048]{3,1,2,0:T(2,128)(2,1)S(1)} copy(bf16[32,2,6,2048]{3,2,1,0:T(8,128)(2,1)} %reshape.317) | data formatting | bytes 3145728 | tf_op jit(solution)/shard_map/reshape | solution.py:160
  92.3 32.3 %all_to_all.10 = bf16[32,2,6,2048]{3,1,2,0:T(2,128)(2,1)S(1)} all-to-all(bf16[32,2,6,2048]{3,1,2,0:T(2,128)(2,1)S(1)} %copy.92), channel_id=1, replica_groups=mesh['dp'=32,'head'=4] {'dp'}, dimensions={0} | all-to-all | bytes 3145728 | tf_op jit(solution)/shard_map/all_to_all | solution.py:159
  124.6 5.9 %fusion.15 = f32[32,2,6,2,352]{4,0,3,2,1:T(8,128)S(1)} fusion(bf16[2,2048,2,352]{1,3,2,0:T(8,128)(2,1)} %param.32, bf16[32,2,6,2048,1]{3,1,2,0,4:T(2,128)(2,1)S(1)} %bitcast.99), kind=kOutput, calls=%fused_computation.17 | convolution fusion | flops 1107296256 | bytes 8421376 | tf_op jit(solution)/shard_map/secd,edkf->seckf/dot_general | solution.py:166
  130.5 2.2 %fusion.11 = bf16[32,2,6,2048]{3,0,2,1:T(8,128)(2,1)} fusion(bf16[2,352,2048]{2,1,0:T(8,128)(2,1)S(1)} %copy-done.12, f32[32,2,6,2,352]{4,0,3,2,1:T(8,128)S(1)} %fusion.15), kind=kOutput, calls=%fused_computation.13 | convolution fusion | flops 555245568 | bytes 5537792 | tf_op jit(solution)/shard_map/secf,efd->secd/dot_general | solution.py:170
  133.0 0.6 pad_clamp_fusion
  133.6 1.1 fusion.78
  134.7 1.6 gather_fusion.1
  136.5 2.9 %fusion.6 = f32[32,2,352]{2,0,1:T(8,128)S(1)} fusion(bf16[2048,2,352]{0,2,1:T(8,128)(2,1)} %param.34, bf16[32,2048]{1,0:T(8,128)(2,1)S(1)} %fusion.38), kind=kOutput, calls=%fused_computation.10 | convolution fusion | flops 92274688 | bytes 3104768 | tf_op jit(solution)/shard_map/dot_general | solution.py:187
  139.5 1.0 convolution_convert_fusion
  140.5 13.6 %reduce-scatter.5.cloned.1.call-done = bf16[32,2,6,512]{3,0,2,1:T(8,128)(2,1)} async-done(((bf16[32,2,6,2048]{3,0,2,1:T(8,128)(2,1)}), bf16[32,2,6,512]{3,0,2,1:T(8,128)(2,1)}) %reduce-scatter.5.cloned.1.call-update) | async-done | bytes 393232 | tf_op jit(solution)/shard_map/reduce_scatter | solution.py:173
  154.2 2.1 %copy.95 = bf16[32,2,6,512]{3,1,2,0:T(2,128)(2,1)} copy(bf16[32,2,6,512]{3,0,2,1:T(8,128)(2,1)} %reduce-scatter.5.cloned.1.call-done) | data formatting | bytes 786432 | tf_op jit(solution)/shard_map/reduce_scatter | solution.py:173
  156.3 8.6 %all-to-all-start.1 = ((bf16[32,2,6,512]{3,1,2,0:T(2,128)(2,1)}), bf16[32,2,6,512]{3,1,2,0:T(2,128)(2,1)S(1)}, u32[]{:S(2)}, u32[]{:S(2)}) async-start(bf16[32,2,6,512]{3,1,2,0:T(2,128)(2,1)} %copy.95), calls=%async_computation.3 | async-start | bytes 786432 | tf_op jit(solution)/shard_map/all_to_all | solution.py:176
  164.9 0.6 multiply_divide_fusion
  165.5 0.8 copy.87
  166.3 8.8 %all-to-all-done.1 = bf16[32,2,6,512]{3,1,2,0:T(2,128)(2,1)S(1)} async-done(((bf16[32,2,6,512]{3,1,2,0:T(2,128)(2,1)}), bf16[32,2,6,512]{3,1,2,0:T(2,128)(2,1)S(1)}, u32[]{:S(2)}, u32[]{:S(2)}) %all-to-all-start.1) | async-done | bytes 393248 | tf_op jit(solution)/shard_map/all_to_all | solution.py:176
  175.1 0.9 copy.96
  175.9 1.2 reshape.318
  177.1 1.8 gather_fusion
  178.9 1.8 reshape.320
  180.7 1.3 multiply_reduce_fusion
  182.0 1.4 add_convert_fusion
  (76 shorter events, 3.1 us)
Async XLA Ops:
  6.5 8.4 %copy-start = (bf16[2048,768]{1,0:T(8,128)(2,1)S(1)}, bf16[2048,768]{1,0:T(8,128)(2,1)}, u32[]{:S(2)}) copy-start(bf16[2048,768]{1,0:T(8,128)(2,1)} %param.20) | copy-start | bytes 9437188
  6.5 71.4 %all-reduce.3.cloned.1.call-start = ((), (), s32[]{:S(2)}) async-start(), calls=%async_computation.4 | async-start | bytes 262144 | tf_op jit(solution)/shard_map/psum | solution.py:129
  9.2 7.6 %copy-start.13 = (s32[32]{0:T(128)S(1)}, s32[32]{0:T(128)}, u32[]{:S(2)}) copy-start(s32[32]{0:T(128)} %param.28) | copy-start | bytes 388
  9.2 15.4 %collective-permute-start.2 = (bf16[32,144]{1,0:T(8,128)(2,1)S(1)}, bf16[32,144]{1,0:T(8,128)(2,1)S(1)}, u32[]{:S(2)}, u32[]{:S(2)}) collective-permute-start(bf16[32,144]{1,0:T(8,128)(2,1)S(1)} %convolution_convert_fusion.4), channel_id=1, source_target_pairs={{0,3},{1,0},{2,1},{3,2},{4,7},{5,4},{6,5},{7,6},{8,11},{9,8},{10,9... | collective-permute-start | bytes 27656 | tf_op jit(solution)/shard_map/ppermute | solution.py:92
  12.9 9.1 %collective-permute-start = (bf16[32,144]{1,0:T(8,128)(2,1)S(1)}, bf16[32,144]{1,0:T(8,128)(2,1)}, u32[]{:S(2)}, u32[]{:S(2)}) collective-permute-start(bf16[32,144]{1,0:T(8,128)(2,1)S(1)} %convolution_convert_fusion.4), channel_id=1, source_target_pairs={{0,1},{1,2},{2,3},{3,0},{4,5},{5,6},{6,7},{7,4},{8,9},{9,10},{10,1... | collective-permute-start | bytes 27656 | tf_op jit(solution)/shard_map/ppermute | solution.py:90
  17.0 2.4 %copy-start.9 = (pred[192]{0:T(512)(128)(4,1)}, pred[192]{0:T(512)(128)(4,1)S(1)}, u32[]{:S(2)}) copy-start(pred[192]{0:T(512)(128)(4,1)S(1)} %eq.65) | copy-start | bytes 580
  22.0 4.0 %collective-permute-start.1 = (bf16[32,144]{1,0:T(8,128)(2,1)}, bf16[32,144]{1,0:T(8,128)(2,1)S(1)}, u32[]{:S(2)}, u32[]{:S(2)}) collective-permute-start(bf16[32,144]{1,0:T(8,128)(2,1)} %collective-permute-done), channel_id=1, source_target_pairs={{0,1},{1,2},{2,3},{3,0},{4,5},{5,6},{6,7},{7,4},{8,9},{9,10},{10,1... | collective-permute-start | bytes 27656 | tf_op jit(solution)/shard_map/ppermute | solution.py:90
  29.3 3.8 %copy-start.1 = (bf16[32,128,576]{1,2,0:T(8,128)(2,1)S(1)}, bf16[32,128,576]{1,2,0:T(8,128)(2,1)}, u32[]{:S(2)}) copy-start(bf16[32,128,576]{1,2,0:T(8,128)(2,1)} %param.26) | copy-start | bytes 14155780
  33.0 1.2 copy-start.6
  33.0 1.8 copy-start.3
  34.3 1.7 copy-start.10
  34.3 1.7 copy-start.11
  34.3 43.7 %copy-start.2 = (bf16[32,2048]{1,0:T(8,128)(2,1)S(1)}, bf16[32,2048]{1,0:T(8,128)(2,1)}, u32[]{:S(2)}) copy-start(bf16[32,2048]{1,0:T(8,128)(2,1)} %param.18) | copy-start | bytes 393220
  34.3 45.3 %copy-start.8 = (f32[2048]{0:T(1024)S(1)}, f32[2048]{0:T(1024)}, u32[]{:S(2)}) copy-start(f32[2048]{0:T(1024)} %param.29) | copy-start | bytes 24580
  36.0 118.2 %reduce-scatter.5.cloned.1.call-start = ((), (), s32[]{:S(2)}) async-start(), calls=%async_computation.6 | async-start | bytes 1966080 | tf_op jit(solution)/shard_map/reduce_scatter | solution.py:173
  79.0 0.6 copy-start.5
  124.6 5.9 %copy-start.12 = (bf16[2,352,2048]{2,1,0:T(8,128)(2,1)S(1)}, bf16[2,352,2048]{2,1,0:T(8,128)(2,1)}, u32[]{:S(2)}) copy-start(bf16[2,352,2048]{2,1,0:T(8,128)(2,1)} %param.33) | copy-start | bytes 8650756
  130.5 2.3 %copy-start.7 = (s32[32,6]{0,1:T(8,128)S(1)}, s32[32,6]{0,1:T(8,128)}, u32[]{:S(2)}) copy-start(s32[32,6]{0,1:T(8,128)} %param.31) | copy-start | bytes 2308
  130.5 3.1 %copy-start.14 = (s32[32]{0:T(128)S(1)}, s32[32]{0:T(128)}, u32[]{:S(2)}) copy-start(s32[32]{0:T(128)} %param.28) | copy-start | bytes 388
  132.7 49.3 %reduce-scatter.3.cloned.1.call-start = ((), (), s32[]{:S(2)}) async-start(), calls=%async_computation.5 | async-start | bytes 163840 | tf_op jit(solution)/shard_map/reduce_scatter | solution.py:194
  136.5 3.0 %copy-start.4 = (bf16[352,2048]{1,0:T(8,128)(2,1)S(1)}, bf16[352,2048]{1,0:T(8,128)(2,1)}, u32[]{:S(2)}) copy-start(bf16[352,2048]{1,0:T(8,128)(2,1)} %param.35) | copy-start | bytes 4325380
  156.3 18.7 %all-to-all-start.1 = ((bf16[32,2,6,512]{3,1,2,0:T(2,128)(2,1)}), bf16[32,2,6,512]{3,1,2,0:T(2,128)(2,1)S(1)}, u32[]{:S(2)}, u32[]{:S(2)}) async-start(bf16[32,2,6,512]{3,1,2,0:T(2,128)(2,1)} %copy.95), calls=%async_computation.3 | async-start | bytes 786432 | tf_op jit(solution)/shard_map/all_to_all | solution.py:176
Sparse Core Ops, SparseCore 0:
  36.1 41.8 all-reduce.2
  132.8 21.3 reduce-scatter.4
  156.7 19.3 reduce-scatter.2
